TPU v7x, 256 devices: a whole 4x4x8 slice. The times are simulated.
256 devices in a mesh: dp: 16 (over z, x_lo), seq: 16 (over y, x_hi, core).
Axes of the slice: x: 4 (x_hi: 2, x_lo: 2; x = x_hi * 2 + x_lo), y: 4, z: 8, core: 2. Of those that a mesh axis runs over, the one named last changes fastest.
Arguments:
- states: bfloat16 [16, 1024, 4096], P('dp', 'seq'), may hold values from -6 to 6
- kv_weight: bfloat16 [4096, 1536], P('seq'), may hold values from -0.09375 to 0.09375
- queries: bfloat16 [16, 4096, 768], P('dp', 'seq'), may hold values from -150 to 150
- hidden: bfloat16 [16, 4096, 1536], P('dp', 'seq'), may hold values from -3 to 3
- out_proj: bfloat16 [768, 1536], P('seq'), may hold values from -0.21875 to 0.21875
- disc_in: bfloat16 [1536, 1024], replicated, may hold values from -0.15625 to 0.15625
- conv_weight: bfloat16 [41, 64, 1024], replicated, may hold values from -0.125 to 0.125
- score_weight: float32 [1024], replicated, may hold values from -0.1875 to 0.1875
- frame_len: int32 [16], replicated, may hold values from 1024 to 4096, as said below
- state_len: int32 [16], replicated, may hold values from 256 to 1024, as said below
Outputs:
- grad_out_proj: float32 [768, 1536], P('seq')
- loss_mean: float32 [], replicated
Inputs may be any that keep to these rules, and one draw needn't show every extreme that they name: `frame_len`: one clip has all 4096 frames live in every draw. `state_len`: one clip has all 1024 backbone frames live in every draw.
All inputs are finite; a program needn't handle non-finite values.
Results may differ from a plain program's by a relative error of at most 0.005.
Values may be sent and summed in bfloat16 or wider, within the bound.
No kernel may reach another device: no remote copies, remote signals or barrier semaphores. Data moves between devices by JAX's collectives and lax.ppermute only.
A program may use at most 128 MiB of HBM per device.

v0:
```python
import math
import jax
import jax.numpy as jnp
from jax import lax
from jax.sharding import PartitionSpec as P

HEAD_DIM = 128
GROUPS = 16
STRIDE = 4


def with_halo(array, sides, width):
    for axis, dim in sides:
        size, length = (lax.axis_size(axis), array.shape[dim])
        up = [(i, (i + 1) % size) for i in range(size - 1)]
        down = [(j, i) for i, j in up]
        last = lax.slice_in_dim(array, length - width, length, axis=dim)
        initial = lax.slice_in_dim(array, 0, width, axis=dim)
        before = lax.ppermute(last, axis, up)
        after = lax.ppermute(initial, axis, down)
        array = jnp.concatenate([before, array, after], axis=dim)
    return array


def regroup(weight_taps, group_count):
    kernel, group_in, channels = weight_taps.shape
    blocks = weight_taps.reshape(kernel, group_in, group_count, channels // group_count)
    turned = jnp.transpose(blocks, (0, 3, 2, 1)).reshape(kernel, channels // group_count, channels)
    return jnp.flip(turned, 0)


def disc_conv(padded, weight_taps, group_count, stride):
    return lax.conv_general_dilated(
        padded[None],
        weight_taps,
        (stride,),
        "VALID",
        dimension_numbers=("NWC", "WIO", "NWC"),
        feature_group_count=group_count,
        preferred_element_type=jnp.float32,
    )[0]


def disc_back(grad_wide, flipped, group_count, stride, high_pad):
    return lax.conv_general_dilated(
        grad_wide[None],
        flipped,
        (1,),
        [(0, high_pad)],
        lhs_dilation=(stride,),
        dimension_numbers=("NWC", "WIO", "NWC"),
        feature_group_count=group_count,
        preferred_element_type=jnp.float32,
    )[0]


def attend(query, keys_values, live_keys):
    row_count, att_width = query.shape
    head_count = att_width // HEAD_DIM
    query_heads = query.astype(jnp.float32).reshape(row_count, head_count, HEAD_DIM)
    key_heads = keys_values[:, :att_width].reshape(-1, head_count, HEAD_DIM)
    value_heads = keys_values[:, att_width:].reshape(-1, head_count, HEAD_DIM)
    scores = jnp.einsum(
        "qhd,khd->hqk", query_heads, key_heads, precision=lax.Precision.HIGHEST
    ) / math.sqrt(HEAD_DIM)
    scores = jnp.where(live_keys[None, None, :], scores, -1e30)
    row_max = jnp.max(scores, axis=2, keepdims=True)
    expo_scores = jnp.where(live_keys[None, None, :], jnp.exp(scores - row_max), 0.0)
    denom = jnp.sum(expo_scores, axis=2)
    weights = expo_scores.astype(jnp.bfloat16)
    mixed_heads = jnp.einsum(
        "hqk,khd->qhd", weights.astype(jnp.float32), value_heads, precision=lax.Precision.HIGHEST
    )
    mixed_heads = mixed_heads / jnp.transpose(denom)[:, :, None]
    return mixed_heads.reshape(row_count, att_width).astype(jnp.bfloat16)


def shards(
    states,
    kv_weight,
    queries,
    hidden,
    out_proj,
    disc_in,
    conv_weight,
    score_weight,
    frame_len,
    state_len,
):
    states_local = states[0]
    frame_count = hidden.shape[1]
    clip_index = lax.axis_index("dp")
    seq_index = lax.axis_index("seq")
    clip_pick = jnp.arange(frame_len.shape[0]) == clip_index
    clip_frames = jnp.sum(jnp.where(clip_pick, frame_len, 0))
    clip_states = jnp.sum(jnp.where(clip_pick, state_len, 0))
    sliced = states_local
    projected = jnp.dot(
        sliced,
        lax.all_gather(kv_weight, "seq", axis=0, tiled=True),
        preferred_element_type=jnp.float32,
    )
    keys_values = lax.all_gather(projected, "seq", axis=0, tiled=True)
    live_keys = jnp.arange(keys_values.shape[0]) < clip_states
    attended = attend(queries[0], keys_values, live_keys)
    sliced = attended
    lifted = hidden[0].astype(jnp.float32) + jnp.dot(
        sliced,
        lax.all_gather(out_proj, "seq", axis=0, tiled=True),
        preferred_element_type=jnp.float32,
    )
    mixed_rows = lifted.astype(jnp.bfloat16)
    frame_ids = seq_index * frame_count + jnp.arange(frame_count)
    inside = (frame_ids < clip_frames)[:, None]
    disc_feed = jnp.where(
        inside, jnp.dot(mixed_rows, disc_in, preferred_element_type=jnp.float32), 0.0
    ).astype(jnp.bfloat16)
    margin_rows = (conv_weight.shape[0] - 1) // 2
    padded = with_halo(disc_feed, (("seq", 0),), margin_rows)
    pre = disc_conv(padded, conv_weight, GROUPS, STRIDE)
    sigmoid_pre = jax.nn.sigmoid(pre)
    critic = jnp.dot(pre * sigmoid_pre, score_weight, precision=lax.Precision.HIGHEST)
    out_count = pre.shape[0]
    valid_out = STRIDE * (seq_index * out_count + jnp.arange(out_count)) < clip_frames
    shortfall = 1.0 - critic
    local_loss = jnp.sum(jnp.where(valid_out, shortfall * shortfall, 0.0))
    push_score = jnp.where(valid_out, -2.0 * shortfall, 0.0)
    slope_pre = sigmoid_pre * (1.0 + pre * (1.0 - sigmoid_pre))
    grad_pre = (push_score[:, None] * score_weight[None, :] * slope_pre).astype(jnp.bfloat16)
    reach_out = margin_rows // STRIDE
    grad_wide = with_halo(grad_pre, (("seq", 0),), reach_out)
    grad_feed = disc_back(grad_wide, regroup(conv_weight, GROUPS), GROUPS, STRIDE, STRIDE - 1)
    grad_feed = jnp.where(inside, grad_feed, 0.0).astype(jnp.bfloat16)
    grad_mixed = lax.dot_general(
        grad_feed, disc_in, (((1,), (1,)), ((), ())), preferred_element_type=jnp.float32
    ).astype(jnp.bfloat16)
    full_term = lax.dot_general(
        attended, grad_mixed, (((0,), (0,)), ((), ())), preferred_element_type=jnp.float32
    )
    summed_clips = lax.psum(full_term, "dp")
    grad_proj = lax.psum_scatter(summed_clips, "seq", scatter_dimension=0, tiled=True)
    total_loss = lax.psum(local_loss, ("dp", "seq"))
    counted = jnp.sum((frame_len + STRIDE - 1) // STRIDE).astype(jnp.float32)
    return (grad_proj, total_loss / counted)


def solution(mesh):
    return jax.shard_map(
        shards,
        mesh=mesh,
        in_specs=(
            P("dp", "seq", None),
            P("seq", None),
            P("dp", "seq", None),
            P("dp", "seq", None),
            P("seq", None),
            P(),
            P(),
            P(),
            P(),
            P(),
        ),
        out_specs=(P("seq", None), P()),
        check_vma=False,
    )
```

profile of v0, /device:TPU:8, one launch (start us, length us, event | category | flops | bytes accessed | tf_op | source)
XLA Modules:
  0.0 666.0 jit_solution(14477105413284666974)
XLA Ops:
  8.0 100.1 %all-gather.4.cloned.1.call-done = bf16[4096,1536]{1,0:T(8,128)(2,1)} async-done(((bf16[256,1536]{1,0:T(8,128)(2,1)}), bf16[4096,1536]{1,0:T(8,128)(2,1)}) %all-gather.4.cloned.1.call-update) | async-done | bytes 12582928 | tf_op jit(solution)/shard_map/all_gather | solution.py:100
  108.1 7.8 %fusion.31 = f32[64,1536]{1,0:T(8,128)} fusion(bf16[4096,1536]{1,0:T(8,128)(2,1)} %all-gather.4.cloned.1.call-done, bf16[1,64,4096]{2,1,0:T(8,128)(2,1)} %param.10), kind=kOutput, calls=%fused_computation.30 | convolution fusion | flops 805306368 | bytes 13500416 | tf_op jit(solution)/shard_map/dot_general | solution.py:98
  119.9 63.1 %all-gather.6.cloned.1.call-done = f32[1024,1536]{1,0:T(8,128)} async-done(((f32[64,1536]{1,0:T(8,128)}), f32[1024,1536]{1,0:T(8,128)}) %all-gather.6.cloned.1.call-update) | async-done | bytes 6291472 | tf_op jit(solution)/shard_map/all_gather | solution.py:103
  183.0 5.9 fusion.48
  188.9 3.5 copy.19
  192.5 3.6 copy.18
  196.0 4.6 fusion.52
  200.6 2.4 fusion.51
  203.1 1.7 fusion.24
  204.8 33.3 %all-gather.8.cloned.1.call-done = bf16[768,1536]{1,0:T(8,128)(2,1)} async-done(((bf16[48,1536]{1,0:T(8,128)(2,1)}), bf16[768,1536]{1,0:T(8,128)(2,1)}) %all-gather.8.cloned.1.call-update) | async-done | bytes 2359312 | tf_op jit(solution)/shard_map/all_gather | solution.py:109
  238.1 4.3 fusion.23
  243.8 2.2 collective-permute-start
  246.0 5.8 collective-permute-start.1
  251.8 14.8 %shard_map.115 = bf16[41,64,16,64]{3,2,1,0:T(8,128)(2,1)} reshape(bf16[41,64,1024]{2,1,0:T(8,128)(2,1)} %param.16) | data formatting | bytes 10747904 | tf_op jit(solution)/shard_map/shard_map
  266.6 2.0 pad_maximum_fusion
  268.6 2.3 copy.24
  270.9 6.3 copy.25
  277.2 18.9 %fusion.27 = f32[64,16,64]{2,1,0:T(8,128)} fusion(bf16[1,296,16,64]{3,0,2,1:T(2,128)(2,1)} %copy.25, bf16[41,64,16,64]{3,2,1,0:T(8,128)(2,1)} %shard_map.115), kind=kOutput, calls=%fused_computation.25 | convolution fusion | flops 343932928 | bytes 6242304 | tf_op jit(solution)/shard_map/conv_general_dilated | solution.py:33
  299.1 1.9 collective-permute-start.2
  301.0 6.0 collective-permute-start.3
  307.1 19.1 %copy.27 = bf16[41,64,16,64]{1,2,3,0:T(8,128)(2,1)} copy(bf16[41,64,16,64]{3,2,1,0:T(8,128)(2,1)} %shard_map.115) | data formatting | bytes 10747904 | tf_op jit(solution)/shard_map/shard_map
  326.2 15.0 %reshape.48 = bf16[41,64,1024]{2,1,0:T(8,128)(2,1)} reshape(bf16[41,64,16,64]{3,2,1,0:T(8,128)(2,1)} %bitcast.55) | data formatting | bytes 10747904 | tf_op jit(solution)/shard_map/reshape | solution.py:28
  341.2 5.9 rev.6
  347.1 14.8 %rev.7 = bf16[41,64,16,64]{3,2,1,0:T(8,128)(2,1)} reshape(bf16[41,64,1024]{2,1,0:T(8,128)(2,1)} %rev.6) | data formatting | bytes 10747904 | tf_op jit(solution)/shard_map/jit(_flip)/rev | solution.py:29
  363.2 54.6 %fusion.1 = bf16[1,256,16,64]{3,0,2,1:T(2,128)(2,1)} fusion(bf16[1,74,16,64]{3,0,2,1:T(2,128)(2,1)} %broadcast_in_dim.69, bf16[41,64,16,64]{3,2,1,0:T(8,128)(2,1)} %rev.7), kind=kOutput, calls=%fused_computation.1 | convolution fusion | flops 343932928 | bytes 6049792 | tf_op jit(solution)/shard_map/conv_general_dilated | solution.py:45
  417.8 5.7 copy.30
  423.5 2.1 copy.31
  425.5 4.8 fusion.16
  430.4 88.9 %reduce-scatter.2.cloned.1.call-done = f32[48,1536]{1,0:T(8,128)} async-done(((f32[768,1536]{1,0:T(8,128)}), f32[48,1536]{1,0:T(8,128)}) %reduce-scatter.2.cloned.1.call-update) | async-done | bytes 294928 | tf_op jit(solution)/shard_map/reduce_scatter | solution.py:141
  520.0 74.0 %psum.15 = f32[]{:T(128)} all-reduce(f32[]{:T(128)} %get-tuple-element.10), channel_id=1, replica_groups=mesh['dp'=16,'seq'=16] {'dp','seq'}, use_global_device_ids=true, to_apply=%region_7.8 | all-reduce | flops 1 | bytes 8 | tf_op jit(solution)/shard_map/psum | solution.py:142
  594.7 61.6 %all-reduce.2.cloned.1.call-done = f32[48,1536]{1,0:T(8,128)} async-done(((f32[48,1536]{1,0:T(8,128)}), f32[48,1536]{1,0:T(8,128)}) %all-reduce.2.cloned.1.call-update) | async-done | bytes 294928 | tf_op jit(solution)/shard_map/psum | solution.py:140
  656.3 1.7 copy.42
  (43 shorter events, 10.5 us)
Async XLA Ops:
  7.2 231.0 %copy-start = (bf16[1536,1024]{1,0:T(8,128)(2,1)S(1)}, bf16[1536,1024]{1,0:T(8,128)(2,1)}, u32[]{:S(2)}) copy-start(bf16[1536,1024]{1,0:T(8,128)(2,1)} %param.15) | copy-start | bytes 9437188
  7.2 100.9 %all-gather.4.cloned.1.call-start = ((), (), s32[]{:S(2)}) async-start(), calls=%async_computation.1 | async-start | bytes 13369344 | tf_op jit(solution)/shard_map/all_gather | solution.py:100
  7.9 109.9 %copy-start.7 = (s32[16]{0:T(128)S(1)}, s32[16]{0:T(128)}, u32[]{:S(2)}) copy-start(s32[16]{0:T(128)} %param.18) | copy-start | bytes 196
  7.9 109.9 %copy-start.8 = (s32[16]{0:T(128)S(1)}, s32[16]{0:T(128)}, u32[]{:S(2)}) copy-start(s32[16]{0:T(128)} %param.19) | copy-start | bytes 196
  7.9 175.1 %all-gather.6.cloned.1.call-start = ((), (), s32[]{:S(2)}) async-start(), calls=%async_computation.2 | async-start | bytes 6684672 | tf_op jit(solution)/shard_map/all_gather | solution.py:103
  115.9 122.3 %all-gather.8.cloned.1.call-start = ((), (), s32[]{:S(2)}) async-start(), calls=%async_computation.3 | async-start | bytes 2506752 | tf_op jit(solution)/shard_map/all_gather | solution.py:109
  116.6 402.7 %reduce-scatter.2.cloned.1.call-start = ((), (), s32[]{:S(2)}) async-start(), calls=%async_computation.4 | async-start | bytes 5013504 | tf_op jit(solution)/shard_map/reduce_scatter | solution.py:141
  119.2 118.9 %copy-start.5 = (pred[256]{0:T(512)(128)(4,1)}, pred[256]{0:T(512)(128)(4,1)S(1)}, u32[]{:S(2)}) copy-start(pred[256]{0:T(512)(128)(4,1)S(1)} %add_compare_fusion) | copy-start | bytes 772
  200.6 2.4 copy-start.1
  204.8 37.6 %copy-start.2 = (bf16[256,6,128]{0,2,1:T(8,128)(2,1)}, bf16[256,6,128]{0,2,1:T(8,128)(2,1)S(1)}, u32[]{:S(2)}) copy-start(bf16[256,6,128]{0,2,1:T(8,128)(2,1)S(1)} %fusion.24) | copy-start | bytes 1179652
  243.8 22.7 %collective-permute-start = (bf16[20,1024]{1,0:T(8,128)(2,1)}, bf16[20,1024]{1,0:T(8,128)(2,1)S(1)}, u32[]{:S(2)}, u32[]{:S(2)}) collective-permute-start(bf16[20,1024]{1,0:T(8,128)(2,1)} %get-tuple-element.6), channel_id=1, source_target_pairs={{0,1},{1,2},{2,3},{3,4},{4,5},{5,6},{6,7},{7,8},{8,9},{9,10},{10,1... | collective-permute-start | bytes 122888 | tf_op jit(solution)/shard_map/ppermute | solution.py:19
  246.0 20.6 %collective-permute-start.1 = (bf16[20,1024]{1,0:T(8,128)(2,1)}, bf16[20,1024]{1,0:T(8,128)(2,1)S(1)}, u32[]{:S(2)}, u32[]{:S(2)}) collective-permute-start(bf16[20,1024]{1,0:T(8,128)(2,1)} %get-tuple-element.7), channel_id=1, source_target_pairs={{1,0},{2,1},{3,2},{4,3},{5,4},{6,5},{7,6},{8,7},{9,8},{10,9},{11,1... | collective-permute-start | bytes 122888 | tf_op jit(solution)/shard_map/ppermute | solution.py:20
  277.2 20.1 %copy-start.4 = (f32[1024]{0:T(1024)S(1)}, f32[1024]{0:T(1024)}, u32[]{:S(2)}) copy-start(f32[1024]{0:T(1024)} %param.17) | copy-start | bytes 12292
  299.1 62.8 %collective-permute-start.2 = (bf16[5,1024]{1,0:T(8,128)(2,1)S(1)}, bf16[5,1024]{1,0:T(8,128)(2,1)S(1)}, u32[]{:S(2)}, u32[]{:S(2)}) collective-permute-start(bf16[5,1024]{1,0:T(8,128)(2,1)S(1)} %get-tuple-element.8), channel_id=1, source_target_pairs={{0,1},{1,2},{2,3},{3,4},{4,5},{5,6},{6,7},{7,8},{8,9},{9,10},{10,1... | collective-permute-start | bytes 30728 | tf_op jit(solution)/shard_map/ppermute | solution.py:19
  301.0 60.9 %collective-permute-start.3 = (bf16[5,1024]{1,0:T(8,128)(2,1)S(1)}, bf16[5,1024]{1,0:T(8,128)(2,1)S(1)}, u32[]{:S(2)}, u32[]{:S(2)}) collective-permute-start(bf16[5,1024]{1,0:T(8,128)(2,1)S(1)} %get-tuple-element.9), channel_id=1, source_target_pairs={{1,0},{2,1},{3,2},{4,3},{5,4},{6,5},{7,6},{8,7},{9,8},{10,9},{11,1... | collective-permute-start | bytes 30728 | tf_op jit(solution)/shard_map/ppermute | solution.py:20
  417.8 7.7 %copy-start.3 = (bf16[256,6,128]{0,2,1:T(8,128)(2,1)S(1)}, bf16[256,6,128]{0,2,1:T(8,128)(2,1)}, u32[]{:S(2)}) copy-start(bf16[256,6,128]{0,2,1:T(8,128)(2,1)} %copy-done.2) | copy-start | bytes 1179652
  417.8 7.7 %copy-start.6 = (pred[256]{0:T(512)(128)(4,1)S(1)}, pred[256]{0:T(512)(128)(4,1)}, u32[]{:S(2)}) copy-start(pred[256]{0:T(512)(128)(4,1)} %copy-done.5) | copy-start | bytes 772
  430.4 225.9 %all-reduce.2.cloned.1.call-start = ((), (), s32[]{:S(2)}) async-start(), calls=%async_computation.5 | async-start | bytes 589824 | tf_op jit(solution)/shard_map/psum | solution.py:140
Sparse Core Ops, SparseCore 0:
  10.8 97.2 all-gather.3
  116.0 66.9 all-gather.5
  185.8 52.2 all-gather.7
  430.5 88.7 reduce-scatter.1
  522.0 134.2 all-reduce.1
where the time goes:
time: 678 us; the launch traced here: 666 us
  waiting for transfers between devices  348 us (51%)
  local copies, waits for them, and re-layouts  106 us (16%)
  matrix products  98.3 us (14%)
  blocking collectives  74 us (11%)
  between operations  16.8 us (2%)
  starting transfers between devices  16.1 us (2%)
    all_gather x1, waiting for transfers between devices, shards(): lax.all_gather(kv_weight, 'seq', axis=0, tiled=True)  100 us
    reduce_scatter x1, waiting for transfers between devices, shards(): lax.psum_scatter(summed_clips, 'seq', scatter_dimension=0, tiled=True)  88.9 us
    psum x1, blocking collectives, shards(): total_loss = lax.psum(local_loss, ('dp', 'seq'))  74 us
    all_gather x1, waiting for transfers between devices, shards(): keys_values = lax.all_gather(projected, 'seq', axis=0, tiled=True)  63.1 us
    psum x1, waiting for transfers between devices, shards(): summed_clips = lax.psum(full_term, 'dp')  61.6 us
    conv_general_dilated x1, matrix products, disc_back(): lax.conv_general_dilated(grad_wide[None], flipped, (1,), [(0, high_pad)],...  54.6 us
    another operation x2, local copies, waits for them, and re-layouts  33.9 us
    all_gather x1, waiting for transfers between devices, shards(): lax.all_gather(out_proj, 'seq', axis=0, tiled=True)  33.3 us
  transfers between devices with their start and end apart: 9, of which 5 were waited for; matrix products, arithmetic and copies ran while one was open for 14% of the time, Pallas kernels for 0%

commit v1 on v0

--- a/solution.py
+++ b/solution.py
@@ -1,12 +1,22 @@
+import functools
 import math
 import jax
 import jax.numpy as jnp
 from jax import lax
 from jax.sharding import PartitionSpec as P
+from jax.lax import all_gather
 
 HEAD_DIM = 128
 GROUPS = 16
 STRIDE = 4
+
+
+def part_runs(inputs, ax_name):
+    side_arr = all_gather(inputs, ax_name).sum(axis=0)
+    return side_arr
+
+
+direct_case = functools.partial(part_runs, ax_name="dp")
 
 
 def with_halo(array, sides, width):
@@ -137,7 +147,7 @@
     full_term = lax.dot_general(
         attended, grad_mixed, (((0,), (0,)), ((), ())), preferred_element_type=jnp.float32
     )
-    summed_clips = lax.psum(full_term, "dp")
+    summed_clips = direct_case(full_term)
     grad_proj = lax.psum_scatter(summed_clips, "seq", scatter_dimension=0, tiled=True)
     total_loss = lax.psum(local_loss, ("dp", "seq"))
     counted = jnp.sum((frame_len + STRIDE - 1) // STRIDE).astype(jnp.float32)

time: 678 us -> 2100 us (3.10)
  waiting for transfers between devices: 348 us -> 1740 us
  other arithmetic: 6.65 us -> 32.7 us
    all_gather x0 -> x1, waiting for transfers between devices: none -> 1530 us  [part_runs(): side_arr = all_gather(inputs, ax_name).sum(axis=0)]
    reduce_scatter x1, waiting for transfers between devices: 88.9 us -> 14.4 us  [shards(): lax.psum_scatter(summed_clips, 'seq', scatter_dimension=0, tiled=True)]
    psum x1 -> x0, waiting for transfers between devices: 61.6 us -> none  [shards(): summed_clips = lax.psum(full_term, 'dp')]
    reduce_sum x0 -> x1, other arithmetic: none -> 26 us  [part_runs(): side_arr = all_gather(inputs, ax_name).sum(axis=0)]
  transfers between devices with their start and end apart: 9 -> 9, of which waited for: 5 -> 5; matrix products, arithmetic and copies ran while one was open for 14% -> 5% of each run, Pallas kernels for 0% -> 0%
where the time goes in v1:
time: 2100 us; the launch traced here: 2090 us
  waiting for transfers between devices  1740 us (83%)
  local copies, waits for them, and re-layouts  104 us (5%)
  matrix products  98.3 us (5%)
  blocking collectives  75.6 us (4%)
  other arithmetic  32.7 us (2%)
    all_gather x1, waiting for transfers between devices, part_runs(): side_arr = all_gather(inputs, ax_name).sum(axis=0)  1530 us
    all_gather x1, waiting for transfers between devices, shards(): lax.all_gather(kv_weight, 'seq', axis=0, tiled=True)  100 us
    psum x1, blocking collectives, shards(): total_loss = lax.psum(local_loss, ('dp', 'seq'))  75.6 us
    all_gather x1, waiting for transfers between devices, shards(): keys_values = lax.all_gather(projected, 'seq', axis=0, tiled=True)  63.1 us
    conv_general_dilated x1, matrix products, disc_back(): lax.conv_general_dilated(grad_wide[None], flipped, (1,), [(0, high_pad)],...  54.6 us
  transfers between devices with their start and end apart: 9, of which 5 were waited for; matrix products, arithmetic and copies ran while one was open for 5% of the time, Pallas kernels for 0%

profile of v1, /device:TPU:8, one launch (start us, length us, event | category | flops | bytes accessed | tf_op | source)
XLA Modules:
  0.0 2085.2 jit_solution(12646026438519398275)
XLA Ops:
  8.0 100.1 %all-gather.6.cloned.1.call-done = bf16[4096,1536]{1,0:T(8,128)(2,1)} async-done(((bf16[256,1536]{1,0:T(8,128)(2,1)}), bf16[4096,1536]{1,0:T(8,128)(2,1)}) %all-gather.6.cloned.1.call-update) | async-done | bytes 12582928 | tf_op jit(solution)/shard_map/all_gather | solution.py:110
  108.1 7.8 fusion.31
  119.9 63.1 %all-gather.8.cloned.1.call-done = f32[1024,1536]{1,0:T(8,128)} async-done(((f32[64,1536]{1,0:T(8,128)}), f32[1024,1536]{1,0:T(8,128)}) %all-gather.8.cloned.1.call-update) | async-done | bytes 6291472 | tf_op jit(solution)/shard_map/all_gather | solution.py:113
  183.0 5.9 fusion.48
  188.9 3.5 copy.19
  192.5 3.6 copy.18
  196.0 4.6 fusion.52
  200.6 2.4 fusion.51
  203.1 1.7 fusion.24
  204.8 33.3 %all-gather.10.cloned.1.call-done = bf16[768,1536]{1,0:T(8,128)(2,1)} async-done(((bf16[48,1536]{1,0:T(8,128)(2,1)}), bf16[768,1536]{1,0:T(8,128)(2,1)}) %all-gather.10.cloned.1.call-update) | async-done | bytes 2359312 | tf_op jit(solution)/shard_map/all_gather | solution.py:119
  238.1 4.3 fusion.23
  243.8 2.2 collective-permute-start
  246.0 5.8 collective-permute-start.1
  251.8 14.8 shard_map.115
  266.6 2.0 pad_maximum_fusion
  268.6 2.3 copy.24
  270.9 6.3 copy.25
  277.2 18.9 fusion.27
  299.1 1.9 collective-permute-start.2
  301.0 6.0 collective-permute-start.3
  307.1 19.1 copy.27
  326.2 15.0 reshape.48
  341.2 5.9 rev.6
  347.1 14.8 rev.7
  363.2 54.6 %fusion.1 = bf16[1,256,16,64]{3,0,2,1:T(2,128)(2,1)} fusion(bf16[1,74,16,64]{3,0,2,1:T(2,128)(2,1)} %broadcast_in_dim.69, bf16[41,64,16,64]{3,2,1,0:T(8,128)(2,1)} %rev.7), kind=kOutput, calls=%fused_computation.1 | convolution fusion | flops 343932928 | bytes 6049792 | tf_op jit(solution)/shard_map/conv_general_dilated | solution.py:55
  417.8 5.7 copy.30
  423.5 2.0 copy.31
  425.5 4.9 fusion.16
  430.5 1529.4 %all-gather.12.cloned.1.call-done = f32[12288,1536]{1,0:T(8,128)} async-done(((f32[768,1536]{1,0:T(8,128)}), f32[12288,1536]{1,0:T(8,128)}) %all-gather.12.cloned.1.call-update) | async-done | bytes 75497488 | tf_op jit(solution)/shard_map/all_gather | solution.py:15
  1959.8 26.0 %reduce_sum.57 = f32[768,1536]{1,0:T(8,128)} reduce(f32[16,768,1536]{2,1,0:T(8,128)} %bitcast.14, f32[]{:T(128)} %constant.42.clone.1), dimensions={0}, to_apply=%region_4.5 | reduce | flops 17694720 | bytes 80216064 | tf_op jit(solution)/shard_map/reduce_sum | solution.py:15
  1986.6 75.6 %psum.7 = f32[]{:T(128)} all-reduce(f32[]{:T(128)} %get-tuple-element.10), channel_id=1, replica_groups=mesh['dp'=16,'seq'=16] {'dp','seq'}, use_global_device_ids=true, to_apply=%region_7.8 | all-reduce | flops 1 | bytes 8 | tf_op jit(solution)/shard_map/psum | solution.py:152
  2062.8 14.4 reduce-scatter.2.cloned.1.call-done
  (43 shorter events, 10.5 us)
Async XLA Ops:
  7.2 231.0 %copy-start = (bf16[1536,1024]{1,0:T(8,128)(2,1)S(1)}, bf16[1536,1024]{1,0:T(8,128)(2,1)}, u32[]{:S(2)}) copy-start(bf16[1536,1024]{1,0:T(8,128)(2,1)} %param.15) | copy-start | bytes 9437188
  7.2 100.9 %all-gather.6.cloned.1.call-start = ((), (), s32[]{:S(2)}) async-start(), calls=%async_computation.1 | async-start | bytes 13369344 | tf_op jit(solution)/shard_map/all_gather | solution.py:110
  7.9 109.9 %copy-start.7 = (s32[16]{0:T(128)S(1)}, s32[16]{0:T(128)}, u32[]{:S(2)}) copy-start(s32[16]{0:T(128)} %param.18) | copy-start | bytes 196
  7.9 109.9 %copy-start.8 = (s32[16]{0:T(128)S(1)}, s32[16]{0:T(128)}, u32[]{:S(2)}) copy-start(s32[16]{0:T(128)} %param.19) | copy-start | bytes 196
  7.9 175.1 %all-gather.8.cloned.1.call-start = ((), (), s32[]{:S(2)}) async-start(), calls=%async_computation.2 | async-start | bytes 6684672 | tf_op jit(solution)/shard_map/all_gather | solution.py:113
  115.9 122.3 %all-gather.10.cloned.1.call-start = ((), (), s32[]{:S(2)}) async-start(), calls=%async_computation.3 | async-start | bytes 2506752 | tf_op jit(solution)/shard_map/all_gather | solution.py:119
  116.6 1843.2 %all-gather.12.cloned.1.call-start = ((), (), s32[]{:S(2)}) async-start(), calls=%async_computation.5 | async-start | bytes 80216064 | tf_op jit(solution)/shard_map/all_gather | solution.py:15
  119.2 118.9 %copy-start.5 = (pred[256]{0:T(512)(128)(4,1)}, pred[256]{0:T(512)(128)(4,1)S(1)}, u32[]{:S(2)}) copy-start(pred[256]{0:T(512)(128)(4,1)S(1)} %add_compare_fusion) | copy-start | bytes 772
  200.6 2.4 copy-start.1
  204.8 37.6 %copy-start.2 = (bf16[256,6,128]{0,2,1:T(8,128)(2,1)}, bf16[256,6,128]{0,2,1:T(8,128)(2,1)S(1)}, u32[]{:S(2)}) copy-start(bf16[256,6,128]{0,2,1:T(8,128)(2,1)S(1)} %fusion.24) | copy-start | bytes 1179652
  243.8 22.7 %collective-permute-start = (bf16[20,1024]{1,0:T(8,128)(2,1)}, bf16[20,1024]{1,0:T(8,128)(2,1)S(1)}, u32[]{:S(2)}, u32[]{:S(2)}) collective-permute-start(bf16[20,1024]{1,0:T(8,128)(2,1)} %get-tuple-element.6), channel_id=1, source_target_pairs={{0,1},{1,2},{2,3},{3,4},{4,5},{5,6},{6,7},{7,8},{8,9},{9,10},{10,1... | collective-permute-start | bytes 122888 | tf_op jit(solution)/shard_map/ppermute | solution.py:29
  246.0 20.6 collective-permute-start.1
  277.2 20.1 copy-start.4
  299.1 62.8 %collective-permute-start.2 = (bf16[5,1024]{1,0:T(8,128)(2,1)S(1)}, bf16[5,1024]{1,0:T(8,128)(2,1)S(1)}, u32[]{:S(2)}, u32[]{:S(2)}) collective-permute-start(bf16[5,1024]{1,0:T(8,128)(2,1)S(1)} %get-tuple-element.8), channel_id=1, source_target_pairs={{0,1},{1,2},{2,3},{3,4},{4,5},{5,6},{6,7},{7,8},{8,9},{9,10},{10,1... | collective-permute-start | bytes 30728 | tf_op jit(solution)/shard_map/ppermute | solution.py:29
  301.0 60.9 %collective-permute-start.3 = (bf16[5,1024]{1,0:T(8,128)(2,1)S(1)}, bf16[5,1024]{1,0:T(8,128)(2,1)S(1)}, u32[]{:S(2)}, u32[]{:S(2)}) collective-permute-start(bf16[5,1024]{1,0:T(8,128)(2,1)S(1)} %get-tuple-element.9), channel_id=1, source_target_pairs={{1,0},{2,1},{3,2},{4,3},{5,4},{6,5},{7,6},{8,7},{9,8},{10,9},{11,1... | collective-permute-start | bytes 30728 | tf_op jit(solution)/shard_map/ppermute | solution.py:30
  417.8 7.7 copy-start.3
  417.8 7.7 copy-start.6
  430.4 1646.8 %reduce-scatter.2.cloned.1.call-start = ((), (), s32[]{:S(2)}) async-start(), calls=%async_computation.4 | async-start | bytes 5013504 | tf_op jit(solution)/shard_map/reduce_scatter | solution.py:151
Sparse Core Ops, SparseCore 0:
  10.8 97.2 all-gather.5
  116.0 66.9 all-gather.7
  185.8 52.2 all-gather.9
  430.5 1529.2 all-gather.11
  1986.0 91.0 reduce-scatter.1
